TPU v7x, 128 devices: a whole 4x4x4 slice. The times are simulated.
128 devices in a mesh: rows: 16 (over x, y_hi, core), cols: 8 (over y_lo, z).
Axes of the slice: x: 4, y: 4 (y_hi: 2, y_lo: 2; y = y_hi * 2 + y_lo), z: 4, core: 2. Of those that a mesh axis runs over, the one named last changes fastest.
Arguments:
- first_profiles: float32 [2048, 65536], P('rows', 'cols'), may hold values from -6 to 6
- second_profiles: float32 [256, 65536], P('rows', 'cols'), may hold values from -6 to 6
- pivot_ids: int32 [16], replicated, may hold values from 0 to 2047
- pivot_corr: float32 [16, 2048], P('cols', 'rows'), may hold values from -0.9 to 0.9
- pair_corr: float32 [2048, 256], P('rows'), may hold values from -0.9 to 0.9
Outputs:
- comoments: float32 [16, 2048, 256], P('cols', 'rows')
All inputs are finite; a program needn't handle non-finite values.
Results may differ from a plain program's by a relative error of at most 0.00007.
Values sent between devices are 32-bit elements; how exact they have to be, the bound alone decides.
A program may use at most 64 MiB of HBM per device.

v0:
```python
import math

import jax
import jax.numpy as jnp
from jax import lax
from jax.sharding import PartitionSpec as P


def total_of_pieces(array, axis):
    parts = lax.all_gather(array, axis)
    return parts.sum(axis=0)


def passed_along(array, axis, by):
    length = lax.axis_size(axis)
    return lax.ppermute(array, axis, [(i, (i + by) % length) for i in range(length)])


def cut_along(array, dim, length):
    shape = array.shape
    parts = array.reshape(*shape[:dim], length, shape[dim] // length, *shape[dim + 1 :])
    return jnp.moveaxis(parts, dim, 0)


def sum_at_owner(array, axis, dim):
    length = lax.axis_size(axis)
    parts = lax.all_to_all(cut_along(array, dim, length), axis, 0, 0, tiled=True)
    return jnp.sum(parts, axis=0)


def shards(first_profiles, second_profiles, pivot_ids, pivot_corr, pair_corr):
    n_rows = lax.axis_size("rows")
    n_cols = lax.axis_size("cols")
    here = lax.axis_index("rows")
    first_count = first_profiles.shape[0]
    second_count = second_profiles.shape[0]
    sample_count = first_profiles.shape[1]
    pivot_count = pivot_ids.shape[0]
    local_ids = pivot_ids - here * first_count
    onehot = (local_ids[:, None] == jnp.arange(first_count, dtype=jnp.int32)[None, :]).astype(
        jnp.float32
    )
    picked = jnp.dot(
        onehot, first_profiles, precision=lax.Precision.HIGHEST, preferred_element_type=jnp.float32
    )
    pivots = total_of_pieces(picked, "rows")

    def contribute(tile, block, anchor):
        scaled = (pivots[:, None, :] * block[None, :, :]).reshape(
            pivot_count * second_count, sample_count
        )
        partial_tile = lax.dot_general(
            first_profiles,
            scaled,
            (((1,), (1,)), ((), ())),
            precision=lax.Precision.HIGHEST,
            preferred_element_type=jnp.float32,
        )
        partial_tile = partial_tile.reshape(first_count, pivot_count, second_count)
        return lax.dynamic_update_slice_in_dim(tile, partial_tile, anchor * second_count, 2)

    tile = jnp.zeros((first_count, pivot_count, second_count * n_rows), jnp.float32)
    tile = contribute(tile, second_profiles, here)

    def step_two(turn, carry):
        acc, ahead, behind = carry
        ahead = passed_along(ahead, "rows", 1)
        behind = passed_along(behind, "rows", -1)
        acc = contribute(acc, ahead, (here - turn) % n_rows)
        acc = contribute(acc, behind, (here + turn) % n_rows)
        return (acc, ahead, behind)

    tile, ahead_last, behind_last = lax.fori_loop(
        1, n_rows // 2 + 1, step_two, (tile, second_profiles, second_profiles)
    )
    totals = sum_at_owner(tile, "cols", 1)
    root_count = math.sqrt(float(sample_count * n_cols))
    corr_first = jnp.transpose(pivot_corr)[:, :, None]
    scaled_out = totals / (root_count * jnp.sqrt(1.0 + corr_first**2 + pair_corr[:, None, :] ** 2))
    return jnp.transpose(scaled_out, (1, 0, 2))


def solution(mesh):
    in_specs = (P("rows", "cols"), P("rows", "cols"), P(), P("cols", "rows"), P("rows", None))
    out_specs = P("cols", "rows", None)
    return jax.shard_map(shards, mesh=mesh, in_specs=in_specs, out_specs=out_specs, check_vma=False)
```

profile of v0, /device:TPU:0, one launch (start us, length us, event | category | flops | bytes accessed | tf_op | source)
XLA Modules:
  0.0 427.8 jit_solution(4288357483261873171)
XLA Ops:
  12.8 75.3 %all-gather.3.cloned.1.call-done = f32[256,8192]{1,0:T(8,128)} async-done(((f32[16,8192]{1,0:T(8,128)}), f32[256,8192]{1,0:T(8,128)}) %all-gather.3.cloned.1.call-update) | async-done | bytes 8388624 | tf_op jit(solution)/shard_map/all_gather | solution.py:10
  94.1 6.7 %fusion.4 = f32[256,128]{1,0:T(8,128)S(1)} fusion(f32[256,8192]{1,0:T(8,128)S(1)} %bitcast.43, f32[128,8192]{1,0:T(8,128)S(1)} %copy-done), kind=kOutput, calls=%fused_computation.14 | convolution fusion | flops 3221225472 | bytes 12713984 | tf_op jit(solution)/shard_map/dot_general | solution.py:52
  103.0 285.9 %while.19 = (s32[]{:T(128)}, f32[128,16,256]{0,2,1:T(8,128)}, f32[16,8192]{1,0:T(8,128)S(1)}, f32[16,8192]{1,0:T(8,128)S(1)}, f32[16,8192]{1,0:T(8,128)S(1)}, /*...) while((s32[]{:T(128)}, f32[128,16,256]{0,2,1:T(8,128)}, ...), condition=%wide.region_2.3_spmd, body=%wide.region_1.2_spmd.sunk | while | flops 6446645248 | bytes 67371560 | solution.py:73
  103.8 6.7 %collective-permute-done = f32[16,8192]{1,0:T(8,128)S(1)} collective-permute-done((f32[16,8192]{1,0:T(8,128)S(1)}, f32[16,8192]{1,0:T(8,128)S(1)}, u32[]{:S(2)}, u32[]{:S(2)}) %collective-permute-start) | collective-permute-done | bytes 524320 | tf_op jit(solution)/shard_map/while/body/eval_jaxpr/ppermute | solution.py:16
  110.5 5.6 %collective-permute-done.1 = f32[16,8192]{1,0:T(8,128)S(1)} collective-permute-done((f32[16,8192]{1,0:T(8,128)S(1)}, f32[16,8192]{1,0:T(8,128)S(1)}, u32[]{:S(2)}, u32[]{:S(2)}) %collective-permute-start.1) | collective-permute-done | bytes 524320 | tf_op jit(solution)/shard_map/while/body/eval_jaxpr/ppermute | solution.py:16
  121.4 9.2 %fusion.22 = f32[256,128]{1,0:T(8,128)S(1)} fusion(f32[256,8192]{1,0:T(8,128)} %bitcast.42, f32[128,8192]{1,0:T(8,128)S(1)} %copy-done.1), kind=kOutput, calls=%fused_computation.12.clone.1 | convolution fusion | flops 3221225472 | bytes 12713984 | tf_op jit(solution)/shard_map/while/body/eval_jaxpr/dot_general | solution.py:52
  130.6 6.7 %fusion.23 = f32[256,128]{1,0:T(8,128)S(1)} fusion(f32[256,8192]{1,0:T(8,128)S(1)} %bitcast.41, f32[128,8192]{1,0:T(8,128)S(1)} %copy-done.1), kind=kOutput, calls=%fused_computation.13.clone.1 | convolution fusion | flops 3221225472 | bytes 12713984 | tf_op jit(solution)/shard_map/while/body/eval_jaxpr/dot_general | solution.py:52
  145.5 6.5 %collective-permute-done.1 = f32[16,8192]{1,0:T(8,128)S(1)} collective-permute-done((f32[16,8192]{1,0:T(8,128)S(1)}, f32[16,8192]{1,0:T(8,128)S(1)}, u32[]{:S(2)}, u32[]{:S(2)}) %collective-permute-start.1) | collective-permute-done | bytes 524320 | tf_op jit(solution)/shard_map/while/body/eval_jaxpr/ppermute | solution.py:16
  157.3 9.2 %fusion.22 = f32[256,128]{1,0:T(8,128)S(1)} fusion(f32[256,8192]{1,0:T(8,128)} %bitcast.42, f32[128,8192]{1,0:T(8,128)S(1)} %copy-done.1), kind=kOutput, calls=%fused_computation.12.clone.1 | convolution fusion | flops 3221225472 | bytes 12713984 | tf_op jit(solution)/shard_map/while/body/eval_jaxpr/dot_general | solution.py:52
  166.5 6.7 %fusion.23 = f32[256,128]{1,0:T(8,128)S(1)} fusion(f32[256,8192]{1,0:T(8,128)S(1)} %bitcast.41, f32[128,8192]{1,0:T(8,128)S(1)} %copy-done.1), kind=kOutput, calls=%fused_computation.13.clone.1 | convolution fusion | flops 3221225472 | bytes 12713984 | tf_op jit(solution)/shard_map/while/body/eval_jaxpr/dot_general | solution.py:52
  181.4 5.7 %collective-permute-done.1 = f32[16,8192]{1,0:T(8,128)S(1)} collective-permute-done((f32[16,8192]{1,0:T(8,128)S(1)}, f32[16,8192]{1,0:T(8,128)S(1)}, u32[]{:S(2)}, u32[]{:S(2)}) %collective-permute-start.1) | collective-permute-done | bytes 524320 | tf_op jit(solution)/shard_map/while/body/eval_jaxpr/ppermute | solution.py:16
  192.4 9.2 %fusion.22 = f32[256,128]{1,0:T(8,128)S(1)} fusion(f32[256,8192]{1,0:T(8,128)} %bitcast.42, f32[128,8192]{1,0:T(8,128)S(1)} %copy-done.1), kind=kOutput, calls=%fused_computation.12.clone.1 | convolution fusion | flops 3221225472 | bytes 12713984 | tf_op jit(solution)/shard_map/while/body/eval_jaxpr/dot_general | solution.py:52
  201.6 6.7 %fusion.23 = f32[256,128]{1,0:T(8,128)S(1)} fusion(f32[256,8192]{1,0:T(8,128)S(1)} %bitcast.41, f32[128,8192]{1,0:T(8,128)S(1)} %copy-done.1), kind=kOutput, calls=%fused_computation.13.clone.1 | convolution fusion | flops 3221225472 | bytes 12713984 | tf_op jit(solution)/shard_map/while/body/eval_jaxpr/dot_general | solution.py:52
  216.6 6.3 %collective-permute-done.1 = f32[16,8192]{1,0:T(8,128)S(1)} collective-permute-done((f32[16,8192]{1,0:T(8,128)S(1)}, f32[16,8192]{1,0:T(8,128)S(1)}, u32[]{:S(2)}, u32[]{:S(2)}) %collective-permute-start.1) | collective-permute-done | bytes 524320 | tf_op jit(solution)/shard_map/while/body/eval_jaxpr/ppermute | solution.py:16
  228.2 9.2 %fusion.22 = f32[256,128]{1,0:T(8,128)S(1)} fusion(f32[256,8192]{1,0:T(8,128)} %bitcast.42, f32[128,8192]{1,0:T(8,128)S(1)} %copy-done.1), kind=kOutput, calls=%fused_computation.12.clone.1 | convolution fusion | flops 3221225472 | bytes 12713984 | tf_op jit(solution)/shard_map/while/body/eval_jaxpr/dot_general | solution.py:52
  237.4 6.7 %fusion.23 = f32[256,128]{1,0:T(8,128)S(1)} fusion(f32[256,8192]{1,0:T(8,128)S(1)} %bitcast.41, f32[128,8192]{1,0:T(8,128)S(1)} %copy-done.1), kind=kOutput, calls=%fused_computation.13.clone.1 | convolution fusion | flops 3221225472 | bytes 12713984 | tf_op jit(solution)/shard_map/while/body/eval_jaxpr/dot_general | solution.py:52
  245.6 5.4 %collective-permute-start.1 = (f32[16,8192]{1,0:T(8,128)S(1)}, f32[16,8192]{1,0:T(8,128)S(1)}, u32[]{:S(2)}, u32[]{:S(2)}) collective-permute-start(f32[16,8192]{1,0:T(8,128)S(1)} %get-tuple-element.260), channel_id=1, source_target_pairs={{0,8},{8,16},{16,24},{24,32},{32,40},{40,48},{48,56},{56,64},{64,7... | collective-permute-start | bytes 1572872 | tf_op jit(solution)/shard_map/while/body/eval_jaxpr/ppermute | solution.py:16
  252.3 5.7 %collective-permute-done.1 = f32[16,8192]{1,0:T(8,128)S(1)} collective-permute-done((f32[16,8192]{1,0:T(8,128)S(1)}, f32[16,8192]{1,0:T(8,128)S(1)}, u32[]{:S(2)}, u32[]{:S(2)}) %collective-permute-start.1) | collective-permute-done | bytes 524320 | tf_op jit(solution)/shard_map/while/body/eval_jaxpr/ppermute | solution.py:16
  263.3 9.2 %fusion.22 = f32[256,128]{1,0:T(8,128)S(1)} fusion(f32[256,8192]{1,0:T(8,128)} %bitcast.42, f32[128,8192]{1,0:T(8,128)S(1)} %copy-done.1), kind=kOutput, calls=%fused_computation.12.clone.1 | convolution fusion | flops 3221225472 | bytes 12713984 | tf_op jit(solution)/shard_map/while/body/eval_jaxpr/dot_general | solution.py:52
  272.5 6.7 %fusion.23 = f32[256,128]{1,0:T(8,128)S(1)} fusion(f32[256,8192]{1,0:T(8,128)S(1)} %bitcast.41, f32[128,8192]{1,0:T(8,128)S(1)} %copy-done.1), kind=kOutput, calls=%fused_computation.13.clone.1 | convolution fusion | flops 3221225472 | bytes 12713984 | tf_op jit(solution)/shard_map/while/body/eval_jaxpr/dot_general | solution.py:52
  280.7 5.4 %collective-permute-start.1 = (f32[16,8192]{1,0:T(8,128)S(1)}, f32[16,8192]{1,0:T(8,128)S(1)}, u32[]{:S(2)}, u32[]{:S(2)}) collective-permute-start(f32[16,8192]{1,0:T(8,128)S(1)} %get-tuple-element.260), channel_id=1, source_target_pairs={{0,8},{8,16},{16,24},{24,32},{32,40},{40,48},{48,56},{56,64},{64,7... | collective-permute-start | bytes 1572872 | tf_op jit(solution)/shard_map/while/body/eval_jaxpr/ppermute | solution.py:16
  287.5 6.3 %collective-permute-done.1 = f32[16,8192]{1,0:T(8,128)S(1)} collective-permute-done((f32[16,8192]{1,0:T(8,128)S(1)}, f32[16,8192]{1,0:T(8,128)S(1)}, u32[]{:S(2)}, u32[]{:S(2)}) %collective-permute-start.1) | collective-permute-done | bytes 524320 | tf_op jit(solution)/shard_map/while/body/eval_jaxpr/ppermute | solution.py:16
  299.1 9.2 %fusion.22 = f32[256,128]{1,0:T(8,128)S(1)} fusion(f32[256,8192]{1,0:T(8,128)} %bitcast.42, f32[128,8192]{1,0:T(8,128)S(1)} %copy-done.1), kind=kOutput, calls=%fused_computation.12.clone.1 | convolution fusion | flops 3221225472 | bytes 12713984 | tf_op jit(solution)/shard_map/while/body/eval_jaxpr/dot_general | solution.py:52
  308.3 6.7 %fusion.23 = f32[256,128]{1,0:T(8,128)S(1)} fusion(f32[256,8192]{1,0:T(8,128)S(1)} %bitcast.41, f32[128,8192]{1,0:T(8,128)S(1)} %copy-done.1), kind=kOutput, calls=%fused_computation.13.clone.1 | convolution fusion | flops 3221225472 | bytes 12713984 | tf_op jit(solution)/shard_map/while/body/eval_jaxpr/dot_general | solution.py:52
  323.2 6.8 %collective-permute-done.1 = f32[16,8192]{1,0:T(8,128)S(1)} collective-permute-done((f32[16,8192]{1,0:T(8,128)S(1)}, f32[16,8192]{1,0:T(8,128)S(1)}, u32[]{:S(2)}, u32[]{:S(2)}) %collective-permute-start.1) | collective-permute-done | bytes 524320 | tf_op jit(solution)/shard_map/while/body/eval_jaxpr/ppermute | solution.py:16
  335.3 9.2 %fusion.22 = f32[256,128]{1,0:T(8,128)S(1)} fusion(f32[256,8192]{1,0:T(8,128)} %bitcast.42, f32[128,8192]{1,0:T(8,128)S(1)} %copy-done.1), kind=kOutput, calls=%fused_computation.12.clone.1 | convolution fusion | flops 3221225472 | bytes 12713984 | tf_op jit(solution)/shard_map/while/body/eval_jaxpr/dot_general | solution.py:52
  344.5 6.7 %fusion.23 = f32[256,128]{1,0:T(8,128)S(1)} fusion(f32[256,8192]{1,0:T(8,128)S(1)} %bitcast.41, f32[128,8192]{1,0:T(8,128)S(1)} %copy-done.1), kind=kOutput, calls=%fused_computation.13.clone.1 | convolution fusion | flops 3221225472 | bytes 12713984 | tf_op jit(solution)/shard_map/while/body/eval_jaxpr/dot_general | solution.py:52
  352.7 5.4 %collective-permute-start.1 = (f32[16,8192]{1,0:T(8,128)S(1)}, f32[16,8192]{1,0:T(8,128)S(1)}, u32[]{:S(2)}, u32[]{:S(2)}) collective-permute-start(f32[16,8192]{1,0:T(8,128)S(1)} %get-tuple-element.260), channel_id=1, source_target_pairs={{0,8},{8,16},{16,24},{24,32},{32,40},{40,48},{48,56},{56,64},{64,7... | collective-permute-start | bytes 1572872 | tf_op jit(solution)/shard_map/while/body/eval_jaxpr/ppermute | solution.py:16
  359.5 6.8 %collective-permute-done.1 = f32[16,8192]{1,0:T(8,128)S(1)} collective-permute-done((f32[16,8192]{1,0:T(8,128)S(1)}, f32[16,8192]{1,0:T(8,128)S(1)}, u32[]{:S(2)}, u32[]{:S(2)}) %collective-permute-start.1) | collective-permute-done | bytes 524320 | tf_op jit(solution)/shard_map/while/body/eval_jaxpr/ppermute | solution.py:16
  371.6 9.2 %fusion.22 = f32[256,128]{1,0:T(8,128)S(1)} fusion(f32[256,8192]{1,0:T(8,128)} %bitcast.42, f32[128,8192]{1,0:T(8,128)S(1)} %copy-done.1), kind=kOutput, calls=%fused_computation.12.clone.1 | convolution fusion | flops 3221225472 | bytes 12713984 | tf_op jit(solution)/shard_map/while/body/eval_jaxpr/dot_general | solution.py:52
  380.8 6.7 %fusion.23 = f32[256,128]{1,0:T(8,128)S(1)} fusion(f32[256,8192]{1,0:T(8,128)S(1)} %bitcast.41, f32[128,8192]{1,0:T(8,128)S(1)} %copy-done.1), kind=kOutput, calls=%fused_computation.13.clone.1 | convolution fusion | flops 3221225472 | bytes 12713984 | tf_op jit(solution)/shard_map/while/body/eval_jaxpr/dot_general | solution.py:52
  393.8 26.0 %all-to-all-done = f32[8,128,2,256]{1,3,2,0:T(8,128)S(1)} async-done(((f32[8,128,2,256]{1,3,2,0:T(8,128)}), f32[8,128,2,256]{1,3,2,0:T(8,128)S(1)}, u32[]{:S(2)}, u32[]{:S(2)}) %all-to-all-start) | async-done | bytes 2097184 | tf_op jit(solution)/shard_map/all_to_all | solution.py:27
  (99 shorter events, 106.4 us)
Async XLA Ops:
  6.5 81.5 %all-gather.3.cloned.1.call-start = ((), (), s32[]{:S(2)}) async-start(), calls=%async_computation.1 | async-start | bytes 8912896 | tf_op jit(solution)/shard_map/all_gather | solution.py:10
  91.9 2.2 copy-start
  103.0 7.5 %collective-permute-start = (f32[16,8192]{1,0:T(8,128)S(1)}, f32[16,8192]{1,0:T(8,128)S(1)}, u32[]{:S(2)}, u32[]{:S(2)}) collective-permute-start(f32[16,8192]{1,0:T(8,128)S(1)} %get-tuple-element.261), channel_id=1, source_target_pairs={{0,120},{8,0},{16,8},{24,16},{32,24},{40,32},{48,40},{56,48},{64,5... | collective-permute-start | bytes 1572872 | tf_op jit(solution)/shard_map/while/body/eval_jaxpr/ppermute | solution.py:16
  103.8 12.3 %collective-permute-start.1 = (f32[16,8192]{1,0:T(8,128)S(1)}, f32[16,8192]{1,0:T(8,128)S(1)}, u32[]{:S(2)}, u32[]{:S(2)}) collective-permute-start(f32[16,8192]{1,0:T(8,128)S(1)} %get-tuple-element.260), channel_id=1, source_target_pairs={{0,8},{8,16},{16,24},{24,32},{32,40},{40,48},{48,56},{56,64},{64,7... | collective-permute-start | bytes 1572872 | tf_op jit(solution)/shard_map/while/body/eval_jaxpr/ppermute | solution.py:16
  116.1 5.3 %copy-start.1 = (f32[128,8192]{1,0:T(8,128)S(1)}, f32[128,8192]{1,0:T(8,128)}, u32[]{:S(2)}) copy-start(f32[128,8192]{1,0:T(8,128)} %get-tuple-element.275) | copy-start | bytes 12582916 | tf_op jit(solution)/shard_map/while
  138.7 6.8 %collective-permute-start = (f32[16,8192]{1,0:T(8,128)S(1)}, f32[16,8192]{1,0:T(8,128)S(1)}, u32[]{:S(2)}, u32[]{:S(2)}) collective-permute-start(f32[16,8192]{1,0:T(8,128)S(1)} %get-tuple-element.261), channel_id=1, source_target_pairs={{0,120},{8,0},{16,8},{24,16},{32,24},{40,32},{48,40},{56,48},{64,5... | collective-permute-start | bytes 1572872 | tf_op jit(solution)/shard_map/while/body/eval_jaxpr/ppermute | solution.py:16
  138.8 13.2 %collective-permute-start.1 = (f32[16,8192]{1,0:T(8,128)S(1)}, f32[16,8192]{1,0:T(8,128)S(1)}, u32[]{:S(2)}, u32[]{:S(2)}) collective-permute-start(f32[16,8192]{1,0:T(8,128)S(1)} %get-tuple-element.260), channel_id=1, source_target_pairs={{0,8},{8,16},{16,24},{24,32},{32,40},{40,48},{48,56},{56,64},{64,7... | collective-permute-start | bytes 1572872 | tf_op jit(solution)/shard_map/while/body/eval_jaxpr/ppermute | solution.py:16
  152.0 5.3 %copy-start.1 = (f32[128,8192]{1,0:T(8,128)S(1)}, f32[128,8192]{1,0:T(8,128)}, u32[]{:S(2)}) copy-start(f32[128,8192]{1,0:T(8,128)} %get-tuple-element.275) | copy-start | bytes 12582916 | tf_op jit(solution)/shard_map/while
  174.6 6.8 %collective-permute-start = (f32[16,8192]{1,0:T(8,128)S(1)}, f32[16,8192]{1,0:T(8,128)S(1)}, u32[]{:S(2)}, u32[]{:S(2)}) collective-permute-start(f32[16,8192]{1,0:T(8,128)S(1)} %get-tuple-element.261), channel_id=1, source_target_pairs={{0,120},{8,0},{16,8},{24,16},{32,24},{40,32},{48,40},{56,48},{64,5... | collective-permute-start | bytes 1572872 | tf_op jit(solution)/shard_map/while/body/eval_jaxpr/ppermute | solution.py:16
  174.7 12.4 %collective-permute-start.1 = (f32[16,8192]{1,0:T(8,128)S(1)}, f32[16,8192]{1,0:T(8,128)S(1)}, u32[]{:S(2)}, u32[]{:S(2)}) collective-permute-start(f32[16,8192]{1,0:T(8,128)S(1)} %get-tuple-element.260), channel_id=1, source_target_pairs={{0,8},{8,16},{16,24},{24,32},{32,40},{40,48},{48,56},{56,64},{64,7... | collective-permute-start | bytes 1572872 | tf_op jit(solution)/shard_map/while/body/eval_jaxpr/ppermute | solution.py:16
  187.1 5.3 %copy-start.1 = (f32[128,8192]{1,0:T(8,128)S(1)}, f32[128,8192]{1,0:T(8,128)}, u32[]{:S(2)}) copy-start(f32[128,8192]{1,0:T(8,128)} %get-tuple-element.275) | copy-start | bytes 12582916 | tf_op jit(solution)/shard_map/while
  209.8 6.8 %collective-permute-start = (f32[16,8192]{1,0:T(8,128)S(1)}, f32[16,8192]{1,0:T(8,128)S(1)}, u32[]{:S(2)}, u32[]{:S(2)}) collective-permute-start(f32[16,8192]{1,0:T(8,128)S(1)} %get-tuple-element.261), channel_id=1, source_target_pairs={{0,120},{8,0},{16,8},{24,16},{32,24},{40,32},{48,40},{56,48},{64,5... | collective-permute-start | bytes 1572872 | tf_op jit(solution)/shard_map/while/body/eval_jaxpr/ppermute | solution.py:16
  209.8 13.0 %collective-permute-start.1 = (f32[16,8192]{1,0:T(8,128)S(1)}, f32[16,8192]{1,0:T(8,128)S(1)}, u32[]{:S(2)}, u32[]{:S(2)}) collective-permute-start(f32[16,8192]{1,0:T(8,128)S(1)} %get-tuple-element.260), channel_id=1, source_target_pairs={{0,8},{8,16},{16,24},{24,32},{32,40},{40,48},{48,56},{56,64},{64,7... | collective-permute-start | bytes 1572872 | tf_op jit(solution)/shard_map/while/body/eval_jaxpr/ppermute | solution.py:16
  222.9 5.3 %copy-start.1 = (f32[128,8192]{1,0:T(8,128)S(1)}, f32[128,8192]{1,0:T(8,128)}, u32[]{:S(2)}) copy-start(f32[128,8192]{1,0:T(8,128)} %get-tuple-element.275) | copy-start | bytes 12582916 | tf_op jit(solution)/shard_map/while
  245.5 6.8 %collective-permute-start = (f32[16,8192]{1,0:T(8,128)S(1)}, f32[16,8192]{1,0:T(8,128)S(1)}, u32[]{:S(2)}, u32[]{:S(2)}) collective-permute-start(f32[16,8192]{1,0:T(8,128)S(1)} %get-tuple-element.261), channel_id=1, source_target_pairs={{0,120},{8,0},{16,8},{24,16},{32,24},{40,32},{48,40},{56,48},{64,5... | collective-permute-start | bytes 1572872 | tf_op jit(solution)/shard_map/while/body/eval_jaxpr/ppermute | solution.py:16
  245.6 12.4 %collective-permute-start.1 = (f32[16,8192]{1,0:T(8,128)S(1)}, f32[16,8192]{1,0:T(8,128)S(1)}, u32[]{:S(2)}, u32[]{:S(2)}) collective-permute-start(f32[16,8192]{1,0:T(8,128)S(1)} %get-tuple-element.260), channel_id=1, source_target_pairs={{0,8},{8,16},{16,24},{24,32},{32,40},{40,48},{48,56},{56,64},{64,7... | collective-permute-start | bytes 1572872 | tf_op jit(solution)/shard_map/while/body/eval_jaxpr/ppermute | solution.py:16
  258.0 5.3 %copy-start.1 = (f32[128,8192]{1,0:T(8,128)S(1)}, f32[128,8192]{1,0:T(8,128)}, u32[]{:S(2)}) copy-start(f32[128,8192]{1,0:T(8,128)} %get-tuple-element.275) | copy-start | bytes 12582916 | tf_op jit(solution)/shard_map/while
  280.6 6.9 %collective-permute-start = (f32[16,8192]{1,0:T(8,128)S(1)}, f32[16,8192]{1,0:T(8,128)S(1)}, u32[]{:S(2)}, u32[]{:S(2)}) collective-permute-start(f32[16,8192]{1,0:T(8,128)S(1)} %get-tuple-element.261), channel_id=1, source_target_pairs={{0,120},{8,0},{16,8},{24,16},{32,24},{40,32},{48,40},{56,48},{64,5... | collective-permute-start | bytes 1572872 | tf_op jit(solution)/shard_map/while/body/eval_jaxpr/ppermute | solution.py:16
  280.7 13.1 %collective-permute-start.1 = (f32[16,8192]{1,0:T(8,128)S(1)}, f32[16,8192]{1,0:T(8,128)S(1)}, u32[]{:S(2)}, u32[]{:S(2)}) collective-permute-start(f32[16,8192]{1,0:T(8,128)S(1)} %get-tuple-element.260), channel_id=1, source_target_pairs={{0,8},{8,16},{16,24},{24,32},{32,40},{40,48},{48,56},{56,64},{64,7... | collective-permute-start | bytes 1572872 | tf_op jit(solution)/shard_map/while/body/eval_jaxpr/ppermute | solution.py:16
  293.8 5.3 %copy-start.1 = (f32[128,8192]{1,0:T(8,128)S(1)}, f32[128,8192]{1,0:T(8,128)}, u32[]{:S(2)}) copy-start(f32[128,8192]{1,0:T(8,128)} %get-tuple-element.275) | copy-start | bytes 12582916 | tf_op jit(solution)/shard_map/while
  316.4 6.8 %collective-permute-start = (f32[16,8192]{1,0:T(8,128)S(1)}, f32[16,8192]{1,0:T(8,128)S(1)}, u32[]{:S(2)}, u32[]{:S(2)}) collective-permute-start(f32[16,8192]{1,0:T(8,128)S(1)} %get-tuple-element.261), channel_id=1, source_target_pairs={{0,120},{8,0},{16,8},{24,16},{32,24},{40,32},{48,40},{56,48},{64,5... | collective-permute-start | bytes 1572872 | tf_op jit(solution)/shard_map/while/body/eval_jaxpr/ppermute | solution.py:16
  316.5 13.5 %collective-permute-start.1 = (f32[16,8192]{1,0:T(8,128)S(1)}, f32[16,8192]{1,0:T(8,128)S(1)}, u32[]{:S(2)}, u32[]{:S(2)}) collective-permute-start(f32[16,8192]{1,0:T(8,128)S(1)} %get-tuple-element.260), channel_id=1, source_target_pairs={{0,8},{8,16},{16,24},{24,32},{32,40},{40,48},{48,56},{56,64},{64,7... | collective-permute-start | bytes 1572872 | tf_op jit(solution)/shard_map/while/body/eval_jaxpr/ppermute | solution.py:16
  330.0 5.3 %copy-start.1 = (f32[128,8192]{1,0:T(8,128)S(1)}, f32[128,8192]{1,0:T(8,128)}, u32[]{:S(2)}) copy-start(f32[128,8192]{1,0:T(8,128)} %get-tuple-element.275) | copy-start | bytes 12582916 | tf_op jit(solution)/shard_map/while
  352.7 6.8 %collective-permute-start = (f32[16,8192]{1,0:T(8,128)S(1)}, f32[16,8192]{1,0:T(8,128)S(1)}, u32[]{:S(2)}, u32[]{:S(2)}) collective-permute-start(f32[16,8192]{1,0:T(8,128)S(1)} %get-tuple-element.261), channel_id=1, source_target_pairs={{0,120},{8,0},{16,8},{24,16},{32,24},{40,32},{48,40},{56,48},{64,5... | collective-permute-start | bytes 1572872 | tf_op jit(solution)/shard_map/while/body/eval_jaxpr/ppermute | solution.py:16
  352.7 13.5 %collective-permute-start.1 = (f32[16,8192]{1,0:T(8,128)S(1)}, f32[16,8192]{1,0:T(8,128)S(1)}, u32[]{:S(2)}, u32[]{:S(2)}) collective-permute-start(f32[16,8192]{1,0:T(8,128)S(1)} %get-tuple-element.260), channel_id=1, source_target_pairs={{0,8},{8,16},{16,24},{24,32},{32,40},{40,48},{48,56},{56,64},{64,7... | collective-permute-start | bytes 1572872 | tf_op jit(solution)/shard_map/while/body/eval_jaxpr/ppermute | solution.py:16
  366.3 5.3 %copy-start.1 = (f32[128,8192]{1,0:T(8,128)S(1)}, f32[128,8192]{1,0:T(8,128)}, u32[]{:S(2)}) copy-start(f32[128,8192]{1,0:T(8,128)} %get-tuple-element.275) | copy-start | bytes 12582916 | tf_op jit(solution)/shard_map/while
  388.9 4.8 %copy-start.2 = (f32[128,256]{1,0:T(8,128)S(1)}, f32[128,256]{1,0:T(8,128)}, u32[]{:S(2)}) copy-start(f32[128,256]{1,0:T(8,128)} %param.11) | copy-start | bytes 393220
  388.9 4.9 %copy-start.3 = (f32[2,128]{1,0:T(2,128)S(1)}, f32[2,128]{1,0:T(2,128)}, u32[]{:S(2)}) copy-start(f32[2,128]{1,0:T(2,128)} %param.10) | copy-start | bytes 3076
  388.9 30.9 %all-to-all-start = ((f32[8,128,2,256]{1,3,2,0:T(8,128)}), f32[8,128,2,256]{1,3,2,0:T(8,128)S(1)}, u32[]{:S(2)}, u32[]{:S(2)}) async-start(f32[8,128,2,256]{1,3,2,0:T(8,128)} %bitcast.11), calls=%async_computation | async-start | bytes 4194304 | tf_op jit(solution)/shard_map/all_to_all | solution.py:27
Sparse Core Ops, SparseCore 0:
  12.8 75.1 all-gather.2
where the time goes:
time: 430 us; the launch traced here: 428 us
  waiting for transfers between devices  169 us (39%)
  matrix products  138 us (32%)
  other arithmetic  48 us (11%)
  starting transfers between devices  41.5 us (10%)
  local copies, waits for them, and re-layouts  17 us (4%)
  between operations  13.5 us (3%)
    dot_general x17, matrix products, contribute(): lax.dot_general(first_profiles, scaled, (((1,), (1,)), ((), ())), precisi...  134 us
    all_gather x1, waiting for transfers between devices, total_of_pieces(): parts = lax.all_gather(array, axis)  75.3 us
    ppermute x16, waiting for transfers between devices, passed_along(): lax.ppermute(array, axis, [(i, (i + by) % length) for i in range(length)])  68 us
    mul x9, other arithmetic, contribute(): pivots[:, None, :] * block[None, :, :]  43.3 us
    ppermute x16, starting transfers between devices, passed_along(): lax.ppermute(array, axis, [(i, (i + by) % length) for i in range(length)])  36.7 us
    all_to_all x1, waiting for transfers between devices, sum_at_owner(): lax.all_to_all(cut_along(array, dim, length), axis, 0, 0, tiled=True)  26 us
    dynamic_update_slice x17, local copies, waits for them, and re-layouts, contribute(): lax.dynamic_update_slice_in_dim(tile, partial_tile, anchor * second_count...  11.6 us
  transfers between devices with their start and end apart: 18, of which 18 were waited for; matrix products, arithmetic and copies ran while one was open for 0% of the time, Pallas kernels for 0%

commit v1 on v0

v1 whole, which is shorter than its diff:
```python
import functools
import math

import jax
import jax.numpy as jnp
from jax import lax
from jax.experimental import pallas as pl
from jax.experimental.pallas import tpu as pltpu
from jax.sharding import PartitionSpec as P

MESH = pl.DeviceIdType.MESH
F32 = jnp.float32
BF16 = jnp.bfloat16
NT = (((1,), (1,)), ((), ()))
CHUNKS = 8
PIECES = 4
ORDER = (2, 1, 3, 0)


def halves(x):
    high = x.astype(BF16)
    return high, (x - high.astype(F32)).astype(BF16)


def kernel(
    root,
    ids,
    first_hbm,
    second_hbm,
    corr_ref,
    pair_ref,
    out_ref,
    first,
    blocks,
    high,
    low,
    scaled,
    tot,
    hop1,
    hop2,
    hop3,
    part,
    norm,
    mine,
    other,
    merged,
    gathered,
    pivots,
    load_f,
    load_s,
    s_send,
    s_recv,
    p_send,
    p_recv,
    r_send,
    r_recv,
):
    r, c = lax.axis_index("rows"), lax.axis_index("cols")
    core, chip = r % 2, r // 2
    x, y = chip // 2, chip % 2
    z, w = c % 4, c // 4
    rows, samples = first_hbm.shape
    size = samples // CHUNKS
    piece = samples // PIECES

    def at_chip(other_chip, other_core=None):
        return (other_chip * 2 + (core if other_core is None else other_core), c)

    x_up, x_down, x_far = (x + 1) % 4, (x + 3) % 4, (x + 2) % 4
    to_y = at_chip(x * 2 + 1 - y)
    to_up = at_chip(x_up * 2 + y)
    to_down = at_chip(x_down * 2 + y)
    to_core = at_chip(chip, 1 - core)
    z_up = (r, w * 4 + (z + 1) % 4)
    z_down = (r, w * 4 + (z + 3) % 4)
    to_w = (r, (1 - w) * 4 + z)

    def part_of(q):
        return pl.ds(pl.multiple_of(q * piece, 128), piece)

    def chunk_of(t):
        return pl.ds(pl.multiple_of(t * size, 128), size)

    def get_first(q):
        return pltpu.make_async_copy(
            first_hbm.at[:, part_of(q)], first.at[:, part_of(q)], load_f.at[q]
        )

    def get_second(t):
        return pltpu.make_async_copy(
            second_hbm.at[:, chunk_of(t)], blocks.at[t, core, x, y], load_s.at[t]
        )

    for q in range(PIECES):
        get_first(q).start()
    for t in range(CHUNKS):
        get_second(t).start()

    barrier = pltpu.get_barrier_semaphore()
    peers = [at_chip((chip + i) % 8) for i in range(1, 8)] + [to_core, z_up, z_down, to_w]
    for peer in peers:
        pl.semaphore_signal(barrier, inc=1, device_id=peer, device_id_type=MESH)
    pl.semaphore_wait(barrier, len(peers))

    def s_copy(t, n, ref, peer):
        return pltpu.make_async_remote_copy(
            src_ref=ref,
            dst_ref=ref,
            send_sem=s_send.at[t, n],
            recv_sem=s_recv.at[t, n],
            device_id=peer,
            device_id_type=MESH,
        )

    def s_copies(t):
        own = blocks.at[t, core, x, y]
        pair = blocks.at[t, core, x, 1 - y]
        return (
            s_copy(t, 0, own, to_y),
            s_copy(t, 1, own, to_up),
            s_copy(t, 2, own, to_down),
            s_copy(t, 3, pair, to_up),
            s_copy(t, 4, pair, to_down),
            s_copy(t, 5, blocks.at[t, core, x_down, y], to_up),
            s_copy(t, 6, blocks.at[t, core, x_up, 1 - y], to_down),
            s_copy(t, 7, blocks.at[t, core, x], to_core),
            s_copy(t, 8, blocks.at[t, core, x_down], to_core),
            s_copy(t, 9, blocks.at[t, core, x_up], to_core),
            s_copy(t, 10, blocks.at[t, core, x_far], to_core),
        )

    def s_stage(t, stage):
        copies = s_copies(t)
        if stage == 0:
            get_second(t).wait()
        waits = ((), (0,), (1, 3, 2, 4), (5, 6), (7, 8, 9, 10))[stage]
        starts = ((0, 1, 2), (3, 4, 7), (5, 6, 8, 9), (10,), ())[stage]
        for n in waits:
            copies[n].wait_recv()
        for n in starts:
            copies[n].start()

    def p_copy(q, n, src, dst, peer):
        return pltpu.make_async_remote_copy(
            src_ref=src,
            dst_ref=dst,
            send_sem=p_send.at[q, n],
            recv_sem=p_recv.at[q, n],
            device_id=peer,
            device_id_type=MESH,
        )

    def p_copies(q):
        span = part_of(q)
        first_copy = p_copy(
            q, 0, mine.at[pl.ds(8 * (1 - core), 8), :, span], other.at[:, :, span], to_core
        )
        spread, gather = [], []
        for i in range(1, 8):
            there = (chip + i) % 8
            spread.append(
                p_copy(q, i, merged.at[there, :, span], gathered.at[i, :, span], at_chip(there))
            )
            row = pivots.at[8 * core + chip, :, span]
            gather.append(p_copy(q, 7 + i, row, row, at_chip(there)))
        rows_here = pivots.at[pl.ds(8 * core, 8), :, span]
        last = p_copy(q, 15, rows_here, rows_here, to_core)
        return first_copy, spread, gather, last

    def p_stage(q, stage):
        first_copy, spread, gather, last = p_copies(q)
        span = part_of(q)
        if stage == 0:
            for j in range(16):
                spot = ids[j] - r * rows
                here = jnp.logical_and(spot >= 0, spot < rows)
                row = first[pl.ds(jnp.clip(spot, 0, rows - 1), 1), span]
                mine[j, :, span] = jnp.where(here, row, jnp.zeros_like(row))
            first_copy.start()
        elif stage == 1:
            first_copy.wait_recv()
            merged[:, :, span] = mine[pl.ds(8 * core, 8), :, span] + other[:, :, span]
            for copy in spread:
                copy.start()
        elif stage == 2:
            for copy in spread:
                copy.wait_recv()
            total = merged[chip, :, span]
            for i in range(1, 8):
                total = total + gathered[i, :, span]
            pivots[8 * core + chip, :, span] = total
            for copy in gather:
                copy.start()
        elif stage == 3:
            for copy in gather:
                copy.wait_recv()
            last.start()
        else:
            last.wait_recv()

    s_stage(0, 0)
    for q in range(PIECES):
        get_first(q).wait()
    p_stage(0, 0)
    s_stage(1, 0)
    p_stage(0, 1)
    s_stage(0, 1)
    p_stage(0, 2)
    s_stage(2, 0)
    s_stage(1, 1)
    p_stage(1, 0)
    s_stage(0, 2)
    p_stage(0, 3)
    s_stage(3, 0)
    s_stage(2, 1)
    s_stage(1, 2)
    s_stage(0, 3)
    p_stage(1, 1)
    for p in range(2):
        column = jnp.transpose(jnp.broadcast_to(corr_ref[p : p + 1, :], (rows, rows)))
        column = jnp.concatenate([column] * (pair_ref.shape[1] // rows), 1)
        pair = pair_ref[...]
        norm[p] = 1.0 / (root * jnp.sqrt(1.0 + column * column + pair * pair))
    p_stage(1, 2)
    p_stage(0, 4)

    tot[...] = jnp.zeros_like(tot)

    def index_of(p, d, e):
        return 2 * (((w + e) % 2) * 4 + (z + d) % 4) + p

    def build(slot, t, js):
        span = chunk_of(t)
        for n, j in enumerate(js):
            up, down = halves(first[:, span] * pivots[j, :, span])
            scaled[slot, n * rows : (n + 1) * rows, :size] = up
            scaled[slot, n * rows : (n + 1) * rows, size:] = down

    def product(slot, t, count):
        left = scaled[slot, : count * rows]
        up, down = high[t], low[t]
        left = jnp.concatenate([left, left[:, :size]], 1)
        right = jnp.concatenate([up, up, down], 1)
        return lax.dot_general(left, right, NT, preferred_element_type=F32)

    def main(t, carry):
        for ahead, stage in ((4, 0), (3, 1), (2, 2), (1, 3)):

            @pl.when(t + ahead < CHUNKS)
            def _():
                s_stage(t + ahead, stage)

        q = t // 2

        @pl.when(jnp.logical_and(t % 2 == 0, q + 1 < PIECES))
        def _():
            p_stage(q + 1, 3)

        @pl.when(jnp.logical_and(t % 2 == 0, q + 2 < PIECES))
        def _():
            p_stage(q + 2, 0)

        @pl.when(jnp.logical_and(t % 2 == 1, q + 2 < PIECES))
        def _():
            p_stage(q + 2, 1)

        @pl.when(jnp.logical_and(t % 2 == 1, q + 1 < PIECES))
        def _():
            p_stage(q + 1, 4)

        s_stage(t, 4)
        for n in range(16):
            a, b, k = n // 4, (n // 2) % 2, n % 2
            up, down = halves(blocks[t, k, a, b])
            high[t, n * 16 : (n + 1) * 16, :] = up
            low[t, n * 16 : (n + 1) * 16, :] = down
        for g in range(2):
            ds = ORDER[2 * g : 2 * g + 2]
            build(g, t, [index_of(0, d, e) for d in ds for e in range(2)])
            result = product(g, t, 4)
            for m, d in enumerate(ds):
                for e in range(2):
                    lo = (2 * m + e) * rows
                    tot[0, d, e] += result[lo : lo + rows]

        @pl.when(jnp.logical_and(t % 2 == 1, q + 2 < PIECES))
        def _():
            p_stage(q + 2, 2)

        return carry

    lax.fori_loop(0, CHUNKS, main, 0)

    half = rows // 2

    def r_copy(p, n, src, dst, peer):
        return pltpu.make_async_remote_copy(
            src_ref=src,
            dst_ref=dst,
            send_sem=r_send.at[p, n],
            recv_sem=r_recv.at[p, n],
            device_id=peer,
            device_id_type=MESH,
        )

    def r_copies(p):
        return (
            r_copy(p, 0, tot.at[p, 2, :, pl.ds(0, half)], hop1.at[p, 0], z_up),
            r_copy(p, 1, tot.at[p, 2, :, pl.ds(half, half)], hop1.at[p, 1], z_down),
            r_copy(p, 2, tot.at[p, 1, 1], hop2.at[p, 0, 1], z_up),
            r_copy(p, 3, tot.at[p, 3, 1], hop2.at[p, 1, 1], z_down),
            r_copy(p, 4, tot.at[p, 1, 0], hop2.at[p, 0, 0], z_up),
            r_copy(p, 5, tot.at[p, 3, 0], hop2.at[p, 1, 0], z_down),
            r_copy(p, 6, part.at[p], hop3.at[p], to_w),
        )

    def far_out(p):
        copies = r_copies(p)
        copies[0].start()
        copies[1].start()

    def near_out(p, side):
        copies = r_copies(p)
        copies[side].wait_recv()
        d = (1, 3)[side]
        tot[p, d, :, side * half : (side + 1) * half] += hop1[p, side]
        copies[2 + side].start()
        copies[4 + side].start()

    def pair_out(p):
        copies = r_copies(p)
        copies[2].wait_recv()
        copies[3].wait_recv()
        part[p] = tot[p, 0, 1] + hop2[p, 0, 1] + hop2[p, 1, 1]
        copies[6].start()

    def finish(p):
        copies = r_copies(p)
        copies[4].wait_recv()
        copies[5].wait_recv()
        mine_now = tot[p, 0, 0] + hop2[p, 0, 0] + hop2[p, 1, 0]
        copies[6].wait_recv()
        out_ref[p] = (mine_now + hop3[p]) * norm[p]

    def second_pass(d):
        js = [index_of(1, d, e) for e in range(2)]

        def body(u, carry):
            for g in range(2):
                t = 2 * u + g
                build(g, t, js)
                result = product(g, t, 2)
                for e in range(2):
                    tot[1, d, e] += result[e * rows : (e + 1) * rows]
            return carry

        lax.fori_loop(0, CHUNKS // 2, body, 0)

    far_out(0)
    second_pass(2)
    near_out(0, 0)
    near_out(0, 1)
    far_out(1)
    second_pass(1)
    near_out(1, 0)
    second_pass(3)
    near_out(1, 1)
    pair_out(0)
    second_pass(0)
    pair_out(1)
    finish(0)
    finish(1)

    def drain(t, carry):
        for copy in s_copies(t):
            copy.wait_send()
        return carry

    lax.fori_loop(0, CHUNKS, drain, 0)

    def drain_pivots(q, carry):
        first_copy, spread, gather, last = p_copies(q)
        for copy in (first_copy, *spread, *gather, last):
            copy.wait_send()
        return carry

    lax.fori_loop(0, PIECES, drain_pivots, 0)
    for p in range(2):
        for copy in r_copies(p):
            copy.wait_send()


def shards(first_profiles, second_profiles, pivot_ids, pivot_corr, pair_corr):
    n_cols = lax.axis_size("cols")
    rows, samples = first_profiles.shape
    second_rows = second_profiles.shape[0]
    width = pair_corr.shape[1]
    size = samples // CHUNKS
    root = math.sqrt(float(samples * n_cols))
    vmem = pl.BlockSpec(memory_space=pltpu.VMEM)
    hbm = pl.BlockSpec(memory_space=pl.ANY)
    dma = pltpu.SemaphoreType.DMA
    return pl.pallas_call(
        functools.partial(kernel, root),
        out_shape=jax.ShapeDtypeStruct((2, rows, width), F32),
        in_specs=[pl.BlockSpec(memory_space=pltpu.SMEM), hbm, hbm, vmem, vmem],
        out_specs=vmem,
        scratch_shapes=[
            pltpu.VMEM((rows, samples), F32),
            pltpu.VMEM((CHUNKS, 2, 4, 2, second_rows, size), F32),
            pltpu.VMEM((CHUNKS, width, size), BF16),
            pltpu.VMEM((CHUNKS, width, size), BF16),
            pltpu.VMEM((2, 4 * rows, 2 * size), BF16),
            pltpu.VMEM((2, 4, 2, rows, width), F32),
            pltpu.VMEM((2, 2, 2, rows // 2, width), F32),
            pltpu.VMEM((2, 2, 2, rows, width), F32),
            pltpu.VMEM((2, rows, width), F32),
            pltpu.VMEM((2, rows, width), F32),
            pltpu.VMEM((2, rows, width), F32),
            pltpu.VMEM((16, 1, samples), F32),
            pltpu.VMEM((8, 1, samples), F32),
            pltpu.VMEM((8, 1, samples), F32),
            pltpu.VMEM((8, 1, samples), F32),
            pltpu.VMEM((16, 1, samples), F32),
            dma((PIECES,)),
            dma((CHUNKS,)),
            dma((CHUNKS, 11)),
            dma((CHUNKS, 11)),
            dma((PIECES, 16)),
            dma((PIECES, 16)),
            dma((2, 7)),
            dma((2, 7)),
        ],
        compiler_params=pltpu.CompilerParams(
            collective_id=0, has_side_effects=True, vmem_limit_bytes=56 * 2**20
        ),
        name="comoments",
    )(pivot_ids, first_profiles, second_profiles, pivot_corr, pair_corr)


def solution(mesh):
    in_specs = (P("rows", "cols"), P("rows", "cols"), P(), P("cols", "rows"), P("rows", None))
    out_specs = P("cols", "rows", None)
    return jax.shard_map(shards, mesh=mesh, in_specs=in_specs, out_specs=out_specs, check_vma=False)
```

time: 430 us -> 104 us (0.24)
  waiting for transfers between devices: 169 us -> 0 us
  matrix products: 138 us -> 0 us
  Pallas kernels: 0 us -> 101 us
  other arithmetic: 48 us -> 0 us
  starting transfers between devices: 41.5 us -> 0 us
  local copies, waits for them, and re-layouts: 17 us -> 1.67 us
  between operations: 13.5 us -> 0.01 us
    dot_general x18 -> x0, matrix products: 138 us -> none  [the longest x17 134 us: contribute(): lax.dot_general(first_profiles, scaled, (((1,), (1,)), ((), ())), precisi...]
    pallas_call x0 -> x1, Pallas kernels: none -> 101 us  [shards(): pl.pallas_call(functools.partial(kernel, root), out_shape=jax.ShapeDtypeS...]
    all_gather x1 -> x0, waiting for transfers between devices: 75.3 us -> none  [total_of_pieces(): parts = lax.all_gather(array, axis)]
    ppermute x16 -> x0, waiting for transfers between devices: 68 us -> none  [passed_along(): lax.ppermute(array, axis, [(i, (i + by) % length) for i in range(length)])]
    mul x9 -> x0, other arithmetic: 43.3 us -> none  [contribute(): pivots[:, None, :] * block[None, :, :]]
    ppermute x16 -> x0, starting transfers between devices: 36.7 us -> none  [passed_along(): lax.ppermute(array, axis, [(i, (i + by) % length) for i in range(length)])]
    all_to_all x1 -> x0, waiting for transfers between devices: 26 us -> none  [sum_at_owner(): lax.all_to_all(cut_along(array, dim, length), axis, 0, 0, tiled=True)]
    dynamic_update_slice x17 -> x0, local copies, waits for them, and re-layouts: 11.6 us -> none  [contribute(): lax.dynamic_update_slice_in_dim(tile, partial_tile, anchor * second_count...]
  transfers between devices with their start and end apart: 18 -> 0, of which waited for: 18 -> 0; matrix products, arithmetic and copies ran while one was open for 0% -> 0% of each run, Pallas kernels for 0% -> 0%
where the time goes in v1:
time: 104 us; the launch traced here: 103 us
  Pallas kernels  101 us (97%)
  local copies, waits for them, and re-layouts  1.67 us (2%)
    pallas_call x1, Pallas kernels, shards(): pl.pallas_call(functools.partial(kernel, root), out_shape=jax.ShapeDtypeS...  101 us

profile of v1, /device:TPU:0, one launch (start us, length us, event | category | flops | bytes accessed | tf_op | source)
XLA Modules:
  0.0 103.1 jit_solution(10861477636053291134)
XLA Ops:
  0.0 101.4 %comoments.1 = f32[2,128,256]{2,1,0:T(8,128)} custom-call(s32[16]{0:T(128)} %ids.1, f32[128,8192]{1,0:T(8,128)} %first_hbm.1, f32[16,8192]{1,0:T(8,128)} %second_hbm.1, f32[2,128]{1,0:T(2,128)} %corr_ref.1, f32[128,256]{1,0:T(8,128)} %pair_ref.1), custom_call_target="tpu_custom_call" | custom-call | tf_op jit(solution)/shard_map/comoments/pallas_call | solution.py:403
  101.4 1.7 %copy.7 = f32[2,128,256]{2,1,0:T(8,128)} copy(f32[2,128,256]{2,1,0:T(8,128)} %comoments.1) | data formatting | bytes 524288

commit v2 on v1

v2 whole, which is shorter than its diff:
```python
import functools
import math

import jax
import jax.numpy as jnp
from jax import lax
from jax.experimental import pallas as pl
from jax.experimental.pallas import tpu as pltpu
from jax.sharding import PartitionSpec as P

MESH = pl.DeviceIdType.MESH
F32 = jnp.float32
BF16 = jnp.bfloat16
NT = (((1,), (1,)), ((), ()))
CHUNKS = 8
SMALL = 16
LAGS = ((0, 0), (3, 2), (3, 1), (6, 3), (7, 4), (8, 5), (10, 6))
AHEAD = 10
OPENING = (
    *(0, 1, 2, (), (0, 0), (1, 0), (0, 1), (1, 1), (0,), 3),
    *((0, 2), 4, 5, (0, 3), (1, 2), 6, 7, (0, 4), (1, 3)),
    *(8, (0, 5), 9, (0, 6)),
)
GROUP = (0, 1, 1, 2, 2, 3, 3, 4, 4, 4, 4, 5, 4)
PARTS = ((0, 2), (2, 6))
EARLY = (((0, 2), (0, 1)), ((0, 3), (0, 0)), ((1, 2), (1, 3)))


def halves(x):
    high = x.astype(BF16)
    return high, (x - high.astype(F32)).astype(BF16)


def kernel(
    root,
    ids,
    first_hbm,
    second_hbm,
    corr_ref,
    pair_ref,
    out_hbm,
    first,
    blocks,
    high,
    low,
    scaled,
    tot,
    hop1,
    hop2,
    side,
    far_side,
    part,
    norm,
    mine,
    other,
    merged,
    second,
    near,
    gathered,
    pivots,
    load_f,
    load_s,
    s_send,
    s_recv,
    p_send,
    p_recv,
    r_send,
    r_recv,
):
    r, c = lax.axis_index("rows"), lax.axis_index("cols")
    core, chip = r % 2, r // 2
    x, y = chip // 2, chip % 2
    z, w = c % 4, c // 4
    rows, samples = first_hbm.shape
    size = samples // CHUNKS
    small = samples // SMALL

    def at_chip(other_chip, other_core=None):
        return (other_chip * 2 + (core if other_core is None else other_core), c)

    x_up, x_down, x_far = (x + 1) % 4, (x + 3) % 4, (x + 2) % 4
    to_y = at_chip(x * 2 + 1 - y)
    to_up = at_chip(x_up * 2 + y)
    to_down = at_chip(x_down * 2 + y)
    to_core = at_chip(chip, 1 - core)
    z_up = (r, w * 4 + (z + 1) % 4)
    z_down = (r, w * 4 + (z + 3) % 4)
    to_w = (r, (1 - w) * 4 + z)

    def part_of(q):
        return pl.ds(PARTS[q][0] * size, PARTS[q][1] * size)

    def chunk_of(t):
        return pl.ds(pl.multiple_of(t * size, 128), size)

    def get_first():
        return pltpu.make_async_copy(first_hbm, first, load_f.at[0])

    def get_second(t):
        return pltpu.make_async_copy(
            second_hbm.at[:, pl.ds(pl.multiple_of(t * small, 128), small)], blocks.at[t, core, x, y], load_s.at[0]
        )

    for t in range(SMALL):
        get_second(t).start()
    get_first().start()

    barrier = pltpu.get_barrier_semaphore()
    to_far = at_chip(x_far * 2 + y)
    peers = [to_core, to_y, to_up, to_down, to_far, z_up, z_down, to_w]
    for peer in peers:
        pl.semaphore_signal(barrier, inc=1, device_id=peer, device_id_type=MESH)

    def s_copy(t, n, ref, peer):
        return pltpu.make_async_remote_copy(
            src_ref=ref,
            dst_ref=ref,
            send_sem=s_send.at[t // 8],
            recv_sem=s_recv.at[t, GROUP[n]],
            device_id=peer,
            device_id_type=MESH,
        )

    def s_copies(t):
        own = blocks.at[t, core, x, y]
        pair = blocks.at[t, core, x, 1 - y]
        far = blocks.at[t, core, x_far, y]
        half = own.shape[0] // 2
        return (
            s_copy(t, 0, own, to_y),
            s_copy(t, 1, own, to_up),
            s_copy(t, 2, own, to_down),
            s_copy(t, 3, pair, to_up),
            s_copy(t, 4, pair, to_down),
            s_copy(t, 5, blocks.at[t, core, x_down, y, pl.ds(0, half)], to_up),
            s_copy(t, 6, blocks.at[t, core, x_up, y, pl.ds(half, half)], to_down),
            s_copy(t, 7, blocks.at[t, core, x], to_core),
            s_copy(t, 8, blocks.at[t, core, x_down], to_core),
            s_copy(t, 9, blocks.at[t, core, x_up], to_core),
            s_copy(t, 10, far, to_core),
            s_copy(t, 11, far, to_y),
            s_copy(t, 12, blocks.at[t, core, x_far, 1 - y], to_core),
        )

    def s_stage(t, stage):
        copies = s_copies(t)
        starts = ((0, 1, 2), (3, 4, 7), (5, 6), (11, 10), (8, 9), (12,), ())[stage]
        landed = (
            None,
            (0, blocks.at[t, core, x, 1 - y]),
            (1, blocks.at[t, core, x]),
            (5, blocks.at[t, core, x_far, y]),
            (3, blocks.at[t, core, x]),
            (11, blocks.at[t, core, x_far, 1 - y]),
            (7, blocks.at[t, 1 - core]),
        )[stage]
        if landed:
            s_copy(t, *landed, to_core).wait_recv()
        for n in starts:
            copies[n].start()

    def turn(n):
        for lag, stage in LAGS:
            t = n - lag
            if isinstance(t, int):
                if 0 <= t < SMALL:
                    s_stage(t, stage)
            else:

                @pl.when(jnp.logical_and(t >= 0, t < SMALL))
                def _():
                    s_stage(t, stage)

    def p_copy(q, n, src, dst, peer):
        return pltpu.make_async_remote_copy(
            src_ref=src,
            dst_ref=dst,
            send_sem=p_send.at[0],
            recv_sem=p_recv.at[q, n],
            device_id=peer,
            device_id_type=MESH,
        )

    def p_copies(q):
        span = part_of(q)
        spread, gather = [], []
        row = pivots.at[8 * core + 4 * y + x, :, span]
        for i in range(1, 4):
            there = (x + i) % 4
            peer = at_chip(there * 2 + y)
            spread.append(p_copy(q, 2, near.at[there, :, span], gathered.at[i, :, span], peer))
            gather.append(p_copy(q, 3, row, row, peer))
        pair_rows = pivots.at[pl.ds(8 * core + 4 * y, 4), :, span]
        core_rows = pivots.at[pl.ds(8 * core, 8), :, span]
        return (
            [p_copy(q, 0, mine.at[pl.ds(8 * (1 - core), 8), :, span], other.at[:, :, span], to_core)],
            [p_copy(q, 1, merged.at[pl.ds(4 * (1 - y), 4), :, span], second.at[:, :, span], to_y)],
            spread,
            gather,
            [p_copy(q, 4, pair_rows, pair_rows, to_y)],
            [p_copy(q, 5, core_rows, core_rows, to_core)],
        )

    def p_stage(q, stage):
        copies = p_copies(q)
        span = part_of(q)
        if stage > 0:
            if stage in (3, 4):
                three = gathered.at[pl.ds(1, 3), :, span]
                p_copy(q, stage - 1, three, three, to_core).wait_recv()
            else:
                copies[stage - 1][0].wait_recv()
        if stage == 1:
            merged[:, :, span] = mine[pl.ds(8 * core, 8), :, span] + other[:, :, span]
        elif stage == 2:
            near[:, :, span] = merged[pl.ds(4 * y, 4), :, span] + second[:, :, span]
        elif stage == 3:
            total = near[x, :, span]
            for i in range(1, 4):
                total = total + gathered[i, :, span]
            pivots[8 * core + 4 * y + x, :, span] = total
        if stage < 6:
            for copy in copies[stage]:
                copy.start()

    def prepare():
        tot[...] = jnp.zeros_like(tot)
        for p in range(2):
            column = jnp.transpose(jnp.broadcast_to(corr_ref[p : p + 1, :], (rows, rows)))
            column = jnp.concatenate([column] * (pair_ref.shape[1] // rows), 1)
            pair = pair_ref[...]
            norm[p] = 1.0 / (root * jnp.sqrt(1.0 + column * column + pair * pair))

    def pick():
        get_first().wait()
        for q in range(2):
            span = part_of(q)
            for j in range(16):
                spot = ids[j] - r * rows
                here = jnp.logical_and(spot >= 0, spot < rows)
                row = first[pl.ds(jnp.clip(spot, 0, rows - 1), 1), span]
                mine[j, :, span] = jnp.where(here, row, jnp.zeros_like(row))

    pltpu.make_async_copy(blocks.at[0], blocks.at[0], load_s.at[0]).wait()
    pl.semaphore_wait(barrier, len(peers))

    for step in OPENING:
        if isinstance(step, int):
            turn(step)
        elif step == ():
            pick()
        elif step == (0,):
            prepare()
        else:
            p_stage(*step)

    def index_of(p, d, e):
        return 2 * (((w + e) % 2) * 4 + (z + d) % 4) + p

    def build(slot, t, js):
        span = chunk_of(t)
        for n, j in enumerate(js):
            up, down = halves(first[:, span] * pivots[j, :, span])
            scaled[slot, n * rows : (n + 1) * rows, :size] = up
            scaled[slot, n * rows : (n + 1) * rows, size:] = down

    def product(slot, t, count):
        left = scaled[slot, : count * rows]
        up, down = high[t], low[t]
        left = jnp.concatenate([left, left[:, :size]], 1)
        right = jnp.concatenate([up, up, down], 1)
        return lax.dot_general(left, right, NT, preferred_element_type=F32)

    def main(t, carry):
        turn(2 * t + AHEAD)
        turn(2 * t + AHEAD + 1)

        for when, stage in ((0, 4), (1, 5), (2, 6)):

            @pl.when(t == when)
            def _():
                p_stage(1, stage)

        for n in range(16):
            a, b, k = n // 4, (n // 2) % 2, n % 2
            for m in range(2):
                up, down = halves(blocks[2 * t + m, k, a, b])
                high[t, n * 16 : (n + 1) * 16, m * small : (m + 1) * small] = up
                low[t, n * 16 : (n + 1) * 16, m * small : (m + 1) * small] = down
        for g, group in enumerate(EARLY):
            build(g, t, [index_of(p, d, e) for p, d in group for e in range(2)])
            result = product(g, t, 2 * len(group))
            for m, (p, d) in enumerate(group):
                for e in range(2):
                    lo = (2 * m + e) * rows
                    tot[p, d, e] += result[lo : lo + rows]

        return carry

    lax.fori_loop(0, CHUNKS, main, 0)

    half = rows // 2

    def r_copy(p, n, src, dst, peer, lane=0):
        return pltpu.make_async_remote_copy(
            src_ref=src,
            dst_ref=dst,
            send_sem=r_send.at[p, lane],
            recv_sem=r_recv.at[p, n],
            device_id=peer,
            device_id_type=MESH,
        )

    def f_copies():
        return [r_copy(0, n, tot.at[0, d, 1], side.at[d], to_w) for n, d in enumerate((2, 3, 1, 0))] + [
            r_copy(0, 4, tot.at[0, 2, 0, pl.ds(0, half)], hop1.at[0, 0, 0], z_up, 1),
            r_copy(0, 5, tot.at[0, 2, 0, pl.ds(half, half)], hop1.at[0, 1, 0], z_down, 1),
            r_copy(0, 6, tot.at[0, 1, 0], hop2.at[0, 0, 0], z_up, 1),
            r_copy(0, 7, tot.at[0, 3, 0], hop2.at[0, 1, 0], z_down, 1),
        ]

    def r_copies():
        return (
            r_copy(1, 0, tot.at[1, 2, :, pl.ds(0, half)], hop1.at[1, 0], z_up),
            r_copy(1, 1, tot.at[1, 2, :, pl.ds(half, half)], hop1.at[1, 1], z_down),
            r_copy(1, 2, tot.at[1, 1, 1], hop2.at[1, 0, 1], z_up),
            r_copy(1, 3, tot.at[1, 3, 1], hop2.at[1, 1, 1], z_down),
            r_copy(1, 4, tot.at[1, 1, 0], hop2.at[1, 0, 0], z_up),
            r_copy(1, 5, tot.at[1, 3, 0], hop2.at[1, 1, 0], z_down),
            r_copy(1, 6, part, far_side, to_w, 1),
        )

    def fold_out():
        for copy in f_copies()[:4]:
            copy.start()

    def fold_in(n):
        d = (2, 3, 1, 0)[n]
        copies = f_copies()
        copies[n].wait_recv()
        tot[0, d, 0] += side[d]
        if n == 0:
            copies[4].start()
            copies[5].start()
        if n in (1, 2):
            way = 2 - n
            copies[4 + way].wait_recv()
            tot[0, d, 0, way * half : (way + 1) * half] += hop1[0, way, 0]
            copies[6 + way].start()

    def far_out():
        copies = r_copies()
        copies[0].start()
        copies[1].start()

    def near_out(way):
        copies = r_copies()
        copies[way].wait_recv()
        d = (1, 3)[way]
        tot[1, d, :, way * half : (way + 1) * half] += hop1[1, way]
        copies[2 + way].start()
        copies[4 + way].start()

    def pair_out():
        copies = r_copies()
        copies[2].wait_recv()
        copies[3].wait_recv()
        part[...] = tot[1, 0, 1] + hop2[1, 0, 1] + hop2[1, 1, 1]
        copies[6].start()

    def put_out(p):
        return pltpu.make_async_copy(norm.at[p], out_hbm.at[p], load_f.at[p])

    def finish(p):
        copies = (f_copies(), r_copies())[p]
        for n in ((6, 7), (4, 5))[p]:
            copies[n].wait_recv()
        total = tot[p, 0, 0] + hop2[p, 0, 0] + hop2[p, 1, 0]
        if p == 1:
            copies[6].wait_recv()
            total = total + far_side[...]
        norm[p] = total * norm[p]
        put_out(p).start()

    def second_pass(d):
        js = [index_of(1, d, e) for e in range(2)]

        def body(u, carry):
            for g in range(2):
                t = 2 * u + g
                build(g, t, js)
                result = product(g, t, 2)
                for e in range(2):
                    tot[1, d, e] += result[e * rows : (e + 1) * rows]
            return carry

        lax.fori_loop(0, CHUNKS // 2, body, 0)

    fold_out()
    far_out()
    second_pass(1)
    fold_in(0)
    near_out(0)
    near_out(1)
    second_pass(0)
    fold_in(1)
    fold_in(2)
    for t in (0, 8):
        all_sent = blocks.at[pl.ds(0, 15), 0]
        s_copy(t, 0, all_sent, to_core).wait_send()
    rows_sent = blocks.at[pl.ds(0, 15), 0, 0]
    p_copy(0, 0, rows_sent, rows_sent, to_core).wait_send()
    fold_in(3)
    pair_out()
    finish(0)
    finish(1)
    for p, lane, sent in (
        (0, 0, side),
        (0, 1, side.at[pl.ds(0, 3)]),
        (1, 0, tot.at[0, pl.ds(0, 3)]),
        (1, 1, part),
    ):
        r_copy(p, 0, sent, sent, to_core, lane).wait_send()
    for p in range(2):
        put_out(p).wait()


def shards(first_profiles, second_profiles, pivot_ids, pivot_corr, pair_corr):
    n_cols = lax.axis_size("cols")
    rows, samples = first_profiles.shape
    second_rows = second_profiles.shape[0]
    width = pair_corr.shape[1]
    size = samples // CHUNKS
    small = samples // SMALL
    root = math.sqrt(float(samples * n_cols))
    vmem = pl.BlockSpec(memory_space=pltpu.VMEM)
    hbm = pl.BlockSpec(memory_space=pl.ANY)
    dma = pltpu.SemaphoreType.DMA
    return pl.pallas_call(
        functools.partial(kernel, root),
        out_shape=jax.ShapeDtypeStruct((2, rows, width), F32),
        in_specs=[pl.BlockSpec(memory_space=pltpu.SMEM), hbm, hbm, vmem, vmem],
        out_specs=hbm,
        scratch_shapes=[
            pltpu.VMEM((rows, samples), F32),
            pltpu.VMEM((SMALL, 2, 4, 2, second_rows, small), F32),
            pltpu.VMEM((CHUNKS, width, size), BF16),
            pltpu.VMEM((CHUNKS, width, size), BF16),
            pltpu.VMEM((3, 4 * rows, 2 * size), BF16),
            pltpu.VMEM((2, 4, 2, rows, width), F32),
            pltpu.VMEM((2, 2, 2, rows // 2, width), F32),
            pltpu.VMEM((2, 2, 2, rows, width), F32),
            pltpu.VMEM((4, rows, width), F32),
            pltpu.VMEM((rows, width), F32),
            pltpu.VMEM((rows, width), F32),
            pltpu.VMEM((2, rows, width), F32),
            pltpu.VMEM((16, 1, samples), F32),
            pltpu.VMEM((8, 1, samples), F32),
            pltpu.VMEM((8, 1, samples), F32),
            pltpu.VMEM((4, 1, samples), F32),
            pltpu.VMEM((4, 1, samples), F32),
            pltpu.VMEM((4, 1, samples), F32),
            pltpu.VMEM((16, 1, samples), F32),
            dma((2,)),
            dma((1,)),
            dma((2,)),
            dma((SMALL, 6)),
            dma((1,)),
            dma((2, 6)),
            dma((2, 2)),
            dma((2, 8)),
        ],
        compiler_params=pltpu.CompilerParams(
            collective_id=0, has_side_effects=True, vmem_limit_bytes=56 * 2**20
        ),
        name="comoments",
    )(pivot_ids, first_profiles, second_profiles, pivot_corr, pair_corr)


def solution(mesh):
    in_specs = (P("rows", "cols"), P("rows", "cols"), P(), P("cols", "rows"), P("rows", None))
    out_specs = P("cols", "rows", None)
    return jax.shard_map(shards, mesh=mesh, in_specs=in_specs, out_specs=out_specs, check_vma=False)
```

time: 104 us -> 77.7 us (0.75)
  Pallas kernels: 101 us -> 75.9 us
    pallas_call x1, Pallas kernels: 101 us -> 75.9 us  [shards(): pl.pallas_call(functools.partial(kernel, root), out_shape=jax.ShapeDtypeS...]
where the time goes in v2:
time: 77.7 us; the launch traced here: 77.5 us
  Pallas kernels  75.9 us (98%)
  local copies, waits for them, and re-layouts  1.67 us (2%)
    pallas_call x1, Pallas kernels, shards(): pl.pallas_call(functools.partial(kernel, root), out_shape=jax.ShapeDtypeS...  75.9 us
    unnamed x1, local copies, waits for them, and re-layouts  1.67 us

profile of v2, /device:TPU:0, one launch (start us, length us, event | category | flops | bytes accessed | tf_op | source)
XLA Modules:
  0.0 77.5 jit_solution(9248299159215709453)
XLA Ops:
  0.0 75.9 %comoments.1 = f32[2,128,256]{2,1,0:T(8,128)} custom-call(s32[16]{0:T(128)} %ids.1, f32[128,8192]{1,0:T(8,128)} %first_hbm.1, f32[16,8192]{1,0:T(8,128)} %second_hbm.1, f32[2,128]{1,0:T(2,128)} %corr_ref.1, f32[128,256]{1,0:T(8,128)} %pair_ref.1), custom_call_target="tpu_custom_call" | custom-call | tf_op jit(solution)/shard_map/comoments/pallas_call | solution.py:439
  75.9 1.7 %copy.7 = f32[2,128,256]{2,1,0:T(8,128)} copy(f32[2,128,256]{2,1,0:T(8,128)} %comoments.1) | data formatting | bytes 524288

commit v3 on v2

--- a/solution.py
+++ b/solution.py
@@ -14,12 +14,12 @@
 NT = (((1,), (1,)), ((), ()))
 CHUNKS = 8
 SMALL = 16
-LAGS = ((0, 0), (3, 2), (3, 1), (6, 3), (7, 4), (8, 5), (10, 6))
+LAGS = ((0, 0), (3, 2), (3, 1), (5, 3), (7, 4), (8, 5), (10, 6))
 AHEAD = 10
 OPENING = (
     *(0, 1, 2, (), (0, 0), (1, 0), (0, 1), (1, 1), (0,), 3),
     *((0, 2), 4, 5, (0, 3), (1, 2), 6, 7, (0, 4), (1, 3)),
-    *(8, (0, 5), 9, (0, 6)),
+    *(8, (0, 5), 9, (1, 4), (0, 6)),
 )
 GROUP = (0, 1, 1, 2, 2, 3, 3, 4, 4, 4, 4, 5, 4)
 PARTS = ((0, 2), (2, 6))
@@ -275,7 +275,7 @@
         turn(2 * t + AHEAD)
         turn(2 * t + AHEAD + 1)
 
-        for when, stage in ((0, 4), (1, 5), (2, 6)):
+        for when, stage in ((1, 5), (2, 6)):
 
             @pl.when(t == when)
             def _():

time: 77.7 us -> 75.7 us (0.974)
  Pallas kernels: 75.9 us -> 73.9 us
    pallas_call x1, Pallas kernels: 75.9 us -> 73.9 us  [shards(): pl.pallas_call(functools.partial(kernel, root), out_shape=jax.ShapeDtypeS...]
where the time goes in v3:
time: 75.7 us; the launch traced here: 75.5 us
  Pallas kernels  73.9 us (98%)
  local copies, waits for them, and re-layouts  1.67 us (2%)
    pallas_call x1, Pallas kernels, shards(): pl.pallas_call(functools.partial(kernel, root), out_shape=jax.ShapeDtypeS...  73.9 us
    unnamed x1, local copies, waits for them, and re-layouts  1.67 us

profile of v3, /device:TPU:0, one launch (start us, length us, event | category | flops | bytes accessed | tf_op | source)
XLA Modules:
  0.0 75.5 jit_solution(11389523581665375924)
XLA Ops:
  0.0 73.9 %comoments.1 = f32[2,128,256]{2,1,0:T(8,128)} custom-call(s32[16]{0:T(128)} %ids.1, f32[128,8192]{1,0:T(8,128)} %first_hbm.1, f32[16,8192]{1,0:T(8,128)} %second_hbm.1, f32[2,128]{1,0:T(2,128)} %corr_ref.1, f32[128,256]{1,0:T(8,128)} %pair_ref.1), custom_call_target="tpu_custom_call" | custom-call | tf_op jit(solution)/shard_map/comoments/pallas_call | solution.py:439
  73.9 1.7 %copy.7 = f32[2,128,256]{2,1,0:T(8,128)} copy(f32[2,128,256]{2,1,0:T(8,128)} %comoments.1) | data formatting | bytes 524288

commit v4 on v3

--- a/solution.py
+++ b/solution.py
@@ -14,14 +14,14 @@
 NT = (((1,), (1,)), ((), ()))
 CHUNKS = 8
 SMALL = 16
-LAGS = ((0, 0), (3, 2), (3, 1), (5, 3), (7, 4), (8, 5), (10, 6))
+LAGS = ((3, 2), (5, 3), (0, 0), (3, 1), (8, 4), (10, 5))
 AHEAD = 10
 OPENING = (
     *(0, 1, 2, (), (0, 0), (1, 0), (0, 1), (1, 1), (0,), 3),
     *((0, 2), 4, 5, (0, 3), (1, 2), 6, 7, (0, 4), (1, 3)),
     *(8, (0, 5), 9, (1, 4), (0, 6)),
 )
-GROUP = (0, 1, 1, 2, 2, 3, 3, 4, 4, 4, 4, 5, 4)
+GROUP = (0, 1, 1, 2, 2, 3, 3, 4, 5)
 PARTS = ((0, 2), (2, 6))
 EARLY = (((0, 2), (0, 1)), ((0, 3), (0, 0)), ((1, 2), (1, 3)))
 
@@ -134,28 +134,23 @@
             s_copy(t, 4, pair, to_down),
             s_copy(t, 5, blocks.at[t, core, x_down, y, pl.ds(0, half)], to_up),
             s_copy(t, 6, blocks.at[t, core, x_up, y, pl.ds(half, half)], to_down),
-            s_copy(t, 7, blocks.at[t, core, x], to_core),
-            s_copy(t, 8, blocks.at[t, core, x_down], to_core),
-            s_copy(t, 9, blocks.at[t, core, x_up], to_core),
-            s_copy(t, 10, far, to_core),
-            s_copy(t, 11, far, to_y),
-            s_copy(t, 12, blocks.at[t, core, x_far, 1 - y], to_core),
+            s_copy(t, 7, far, to_y),
+            s_copy(t, 8, blocks.at[t, core], to_core),
         )
 
     def s_stage(t, stage):
         copies = s_copies(t)
-        starts = ((0, 1, 2), (3, 4, 7), (5, 6), (11, 10), (8, 9), (12,), ())[stage]
+        starts = ((0, 1, 2), (3, 4), (5, 6), (7,), (8,), ())[stage]
         landed = (
-            None,
-            (0, blocks.at[t, core, x, 1 - y]),
-            (1, blocks.at[t, core, x]),
-            (5, blocks.at[t, core, x_far, y]),
-            (3, blocks.at[t, core, x]),
-            (11, blocks.at[t, core, x_far, 1 - y]),
-            (7, blocks.at[t, 1 - core]),
+            (),
+            ((0, blocks.at[t, core, x, 1 - y]),),
+            ((1, blocks.at[t, core, x]),),
+            ((5, blocks.at[t, core, x_far, y]),),
+            ((3, blocks.at[t, core, x]), (7, blocks.at[t, core, x_far, 1 - y])),
+            ((8, blocks.at[t, 1 - core]),),
         )[stage]
-        if landed:
-            s_copy(t, *landed, to_core).wait_recv()
+        for arrival in landed:
+            s_copy(t, *arrival, to_core).wait_recv()
         for n in starts:
             copies[n].start()
 

time: 75.7 us -> 74.4 us (0.983)
  Pallas kernels: 73.9 us -> 72.6 us
    pallas_call x1, Pallas kernels: 73.9 us -> 72.6 us  [shards(): pl.pallas_call(functools.partial(kernel, root), out_shape=jax.ShapeDtypeS...]
where the time goes in v4:
time: 74.4 us; the launch traced here: 74.3 us
  Pallas kernels  72.6 us (98%)
  local copies, waits for them, and re-layouts  1.67 us (2%)
    pallas_call x1, Pallas kernels, shards(): pl.pallas_call(functools.partial(kernel, root), out_shape=jax.ShapeDtypeS...  72.6 us
    unnamed x1, local copies, waits for them, and re-layouts  1.67 us

profile of v4, /device:TPU:0, one launch (start us, length us, event | category | flops | bytes accessed | tf_op | source)
XLA Modules:
  0.0 74.3 jit_solution(15801949249728479543)
XLA Ops:
  0.0 72.6 %comoments.1 = f32[2,128,256]{2,1,0:T(8,128)} custom-call(s32[16]{0:T(128)} %ids.1, f32[128,8192]{1,0:T(8,128)} %first_hbm.1, f32[16,8192]{1,0:T(8,128)} %second_hbm.1, f32[2,128]{1,0:T(2,128)} %corr_ref.1, f32[128,256]{1,0:T(8,128)} %pair_ref.1), custom_call_target="tpu_custom_call" | custom-call | tf_op jit(solution)/shard_map/comoments/pallas_call | solution.py:434
  72.6 1.7 %copy.7 = f32[2,128,256]{2,1,0:T(8,128)} copy(f32[2,128,256]{2,1,0:T(8,128)} %comoments.1) | data formatting | bytes 524288

commit v5 on v4

--- a/solution.py
+++ b/solution.py
@@ -381,15 +381,15 @@
         js = [index_of(1, d, e) for e in range(2)]
 
         def body(u, carry):
-            for g in range(2):
-                t = 2 * u + g
-                build(g, t, js)
-                result = product(g, t, 2)
+            for g in range(4):
+                t = 4 * u + g
+                build(g % 3, t, js)
+                result = product(g % 3, t, 2)
                 for e in range(2):
                     tot[1, d, e] += result[e * rows : (e + 1) * rows]
             return carry
 
-        lax.fori_loop(0, CHUNKS // 2, body, 0)
+        lax.fori_loop(0, CHUNKS // 4, body, 0)
 
     fold_out()
     far_out()

time: 74.4 us -> 74.5 us (level)
  no operation moved by 1% of the time
where the time goes in v5:
time: 74.5 us; the launch traced here: 74.4 us
  Pallas kernels  72.7 us (98%)
  local copies, waits for them, and re-layouts  1.67 us (2%)
    pallas_call x1, Pallas kernels, shards(): pl.pallas_call(functools.partial(kernel, root), out_shape=jax.ShapeDtypeS...  72.7 us
    unnamed x1, local copies, waits for them, and re-layouts  1.67 us

profile of v5, /device:TPU:0, one launch (start us, length us, event | category | flops | bytes accessed | tf_op | source)
XLA Modules:
  0.0 74.4 jit_solution(14405632532302687233)
XLA Ops:
  0.0 72.7 %comoments.1 = f32[2,128,256]{2,1,0:T(8,128)} custom-call(s32[16]{0:T(128)} %ids.1, f32[128,8192]{1,0:T(8,128)} %first_hbm.1, f32[16,8192]{1,0:T(8,128)} %second_hbm.1, f32[2,128]{1,0:T(2,128)} %corr_ref.1, f32[128,256]{1,0:T(8,128)} %pair_ref.1), custom_call_target="tpu_custom_call" | custom-call | tf_op jit(solution)/shard_map/comoments/pallas_call | solution.py:434
  72.7 1.7 %copy.7 = f32[2,128,256]{2,1,0:T(8,128)} copy(f32[2,128,256]{2,1,0:T(8,128)} %comoments.1) | data formatting | bytes 524288
